TPU v7x, 512 devices: a whole 4x8x8 slice. The times are simulated.
512 devices in a mesh: dp: 16 (over y, core), table: 32 (over x, z).
Axes of the slice: x: 4, y: 8, z: 8, core: 2. Of those that a mesh axis runs over, the one named last changes fastest.
Arguments:
- bag_slots: int32 [262144, 32], P(('dp', 'table')), may hold values from -1 to 3071
- labels: float32 [262144], P(('dp', 'table')), may hold values from 0 to 1
- cold_ids: int32 [512, 32, 32], P(('dp', 'table')), may hold values from 0 to 1023
- cold_count: int32 [512, 32], P(('dp', 'table')), may hold values from 1 to 32, 512 in all within a row
- table: float32 [32768, 256], P('table'), may hold values from -1.8 to 1.8
- adagrad_sum: float32 [32768], P('table'), may hold values from 0.1 to 10
- hot_ids: int32 [2048], P('table'), may hold values from 0 to 1023
- w_in: bfloat16 [256, 4096], replicated, may hold values from -0.375 to 0.375
- w_out: bfloat16 [4096], replicated, may hold values from -0.09375 to 0.09375
Outputs:
- new_table: float32 [32768, 256], P('table')
- new_sum: float32 [32768], P('table')
Inputs may be any that keep to these rules, and one draw needn't show every extreme that they name: `bag_slots`: -1 marks an empty bag entry. `cold_count`: each reader's counts sum to 512.
All inputs are finite; a program needn't handle non-finite values.
Results may differ from a plain program's by a relative error of at most 0.0045.
The roundings to bfloat16 on the way count: a program that leaves them out, or rounds other values in their place, can miss the bound.
Values may be sent and summed in bfloat16 or wider, within the bound.
A program may use at most 64 MiB of HBM per device.

v0:
```python
import jax
import jax.numpy as jnp
from jax import lax
from jax.sharding import PartitionSpec as P

learning_rate = 0.3


def adagrad_step(own_table, own_sum, grad):
    new_sum = own_sum + jnp.mean(grad * grad, axis=1)
    new_table = own_table - learning_rate * grad / jnp.sqrt(new_sum)[:, None]
    return (new_table, new_sum)


def per_device(bag_slots, labels, cold_ids, cold_count, table, adagrad_sum, hot_ids, w_in, w_out):
    owners = lax.axis_size("table")
    hot_dev = hot_ids.shape[0]
    slot_cap = cold_ids.shape[2]
    batch = bag_slots.shape[0]
    width = table.shape[1]
    hot_cols = owners * hot_dev
    vocab_size = owners * (hot_dev + slot_cap)
    table_bf = table.astype(jnp.bfloat16)
    hot_rows = table_bf[hot_ids]
    sample_ids = jnp.broadcast_to(jnp.arange(batch, dtype=jnp.int32)[:, None], bag_slots.shape)
    column_ids = jnp.where(bag_slots < 0, vocab_size, bag_slots)
    incidence = (
        jnp.zeros((batch, vocab_size), jnp.bfloat16)
        .at[sample_ids, column_ids]
        .add(jnp.ones(bag_slots.shape, jnp.bfloat16), mode="drop")
    )
    hot_incidence = incidence[:, :hot_cols]
    cold_incidence = incidence[:, hot_cols:]
    asked_ids = lax.all_to_all(cold_ids[0], "table", split_axis=0, concat_axis=0, tiled=True)
    served = table_bf[asked_ids]
    fetched = lax.all_to_all(served, "table", split_axis=0, concat_axis=0, tiled=True)
    live_mask = jnp.arange(slot_cap, dtype=jnp.int32)[None, :] < cold_count[0][:, None]
    fetched = jnp.where(live_mask[..., None], fetched, jnp.zeros_like(fetched))
    cold_pooled = jnp.dot(
        cold_incidence, fetched.reshape(-1, width), preferred_element_type=jnp.float32
    )
    columns = hot_incidence
    pooled = (
        cold_pooled
        + jnp.dot(
            columns,
            lax.all_gather(hot_rows, "table", axis=0, tiled=True),
            preferred_element_type=jnp.float32,
        )
    ).astype(jnp.bfloat16)
    pre_act = jnp.dot(pooled, w_in, preferred_element_type=jnp.float32)
    hidden = jax.nn.relu(pre_act).astype(jnp.bfloat16)
    logit = jnp.dot(hidden, w_out, preferred_element_type=jnp.float32)
    dlogit = jax.nn.sigmoid(logit) - labels
    dhidden = (dlogit[:, None] * w_out.astype(jnp.float32)[None, :] * (pre_act > 0)).astype(
        jnp.bfloat16
    )
    dpooled = lax.dot_general(
        dhidden, w_in, (((1,), (1,)), ((), ())), preferred_element_type=jnp.float32
    ).astype(jnp.bfloat16)
    columns = hot_incidence
    hot_grad = lax.psum_scatter(
        lax.dot_general(
            columns, dpooled, (((0,), (0,)), ((), ())), preferred_element_type=jnp.float32
        ).astype(jnp.bfloat16),
        "table",
        scatter_dimension=0,
        tiled=True,
    ).astype(jnp.float32)
    cold_term = lax.dot_general(
        cold_incidence, dpooled, (((0,), (0,)), ((), ())), preferred_element_type=jnp.float32
    )
    cold_term = jnp.where(live_mask[..., None], cold_term.reshape(owners, slot_cap, width), 0.0)
    returned = lax.all_to_all(
        cold_term.astype(jnp.bfloat16), "table", split_axis=0, concat_axis=0, tiled=True
    ).astype(cold_term.dtype)
    grad = jnp.zeros(table.shape, jnp.float32).at[hot_ids].add(hot_grad)
    grad = grad.at[asked_ids.reshape(-1)].add(returned.reshape(-1, width))
    total_grad = lax.psum(grad.astype(jnp.bfloat16), "dp").astype(jnp.float32)
    new_table, new_sum = adagrad_step(table, adagrad_sum, total_grad)
    return (new_table, new_sum)


def solution(mesh):
    placed = (
        P(("dp", "table"), None),
        P(("dp", "table")),
        P(("dp", "table"), None, None),
        P(("dp", "table"), None),
        P("table", None),
        P("table"),
        P("table"),
        P(),
        P(),
    )
    return jax.shard_map(
        per_device,
        mesh=mesh,
        in_specs=placed,
        out_specs=(P("table", None), P("table")),
        check_vma=False,
    )
```

profile of v0, /device:TPU:1, one launch (start us, length us, event | category | flops | bytes accessed | tf_op | source)
XLA Modules:
  0.0 546.6 jit_solution(1328954373111065597)
XLA Ops:
  7.2 0.0 copy-start
  7.2 0.0 all-gather.3.cloned.1.call-start
  7.2 1.4 convert_element_type.35
  8.6 0.0 copy-start.5
  8.7 0.0 copy-start.4
  8.7 0.7 compare_select_fusion.4
  9.4 1.3 gather_fusion.1
  10.7 0.0 copy-start.8
  10.7 0.0 all-gather.3.cloned.1.call-update
  10.7 22.3 %all_to_all.22 = s32[32,1,32]{2,1,0:T(1,128)S(1)} all-to-all(s32[32,1,32]{2,1,0:T(1,128)} %bitcast.24), channel_id=1, replica_groups=mesh['dp'=16,'table'=32] {'table'}, dimensions={0} | all-to-all | bytes 8192 | tf_op jit(solution)/shard_map/all_to_all | solution.py:34
  33.0 0.0 copy-start.9
  33.0 0.1 reshape.131
  33.1 5.0 gather_fusion
  38.1 3.9 all-to-all-start.1
  42.0 0.0 reduce-scatter.2.cloned.1.call-start
  42.0 0.0 copy-done.5
  42.1 0.0 copy-done.4
  42.1 0.0 copy-done.8
  42.1 0.1 multiply_reduce_fusion
  42.2 0.0 copy-done.9
  42.2 0.1 and_reduce_fusion
  42.3 0.1 copy.11
  42.5 0.1 reshape.161
  42.6 114.8 %scatter_custom_fusion.2 = bf16[1572864]{0:T(1024)(128)(2,1)} fusion(s32[16384]{0:T(1024)S(1)} %reshape.161, bf16[16384]{0:T(1024)(128)(2,1)S(1)} %broadcast.91, bf16[]{:T(256)} %constant.12.clone.1), kind=kCustom, calls=%fused_computation.17 | custom fusion | flops 16384 | bytes 3145730
  157.4 0.0 copy-start.10
  157.4 5.8 %reshape.126 = bf16[512,3072]{1,0:T(8,128)(2,1)} reshape(bf16[1572864]{0:T(1024)(128)(2,1)} %scatter_custom_fusion.2) | data formatting | bytes 6291456 | tf_op jit(solution)/shard_map/scatter-add | solution.py:30
  163.2 0.0 copy-done.10
  163.2 0.1 iota_compare_fusion
  163.3 0.0 all-to-all-done.1
  163.3 0.2 broadcast_select_fusion
  163.5 1.7 fusion.28
  165.2 0.0 all-gather.3.cloned.1.call-done
  165.2 0.0 copy-done
  165.2 7.9 %fusion.19 = f32[512,4096]{1,0:T(8,128)} fusion(bf16[256,4096]{1,0:T(8,128)(2,1)S(1)} %copy-done, f32[512,256]{1,0:T(8,128)S(1)} %fusion.28, bf16[2048,256]{1,0:T(8,128)(2,1)} %all-gather.3.cloned.1.call-done, bf16[512,3072]{1,0:T(8,128)(2,1)} %reshape.126), kind=kOutput, calls=%fused_computation.24 | convolution fusion | flops 1610874880 | bytes 14155776 | tf_op jit(solution)/shard_map/dot_general | solution.py:51
  173.2 0.0 copy-start.7
  173.2 0.0 copy-start.1
  173.2 4.7 fusion
  177.9 0.0 copy-done.7
  177.9 1.0 copy-done.1
  178.9 0.0 copy-start.2
  179.0 1.4 fusion.14
  180.4 0.5 copy-done.2
  180.8 1.8 convolution_convert_fusion
  182.6 0.0 reduce-scatter.2.cloned.1.call-update
  182.6 1.7 fusion.26
  184.3 1.0 select_convert_fusion.4
  185.3 0.0 copy-start.6
  185.3 9.5 %all-to-all-start.2 = ((bf16[32,32,256]{2,1,0:T(8,128)(2,1)}), bf16[32,32,256]{2,1,0:T(8,128)(2,1)}, u32[]{:S(2)}, u32[]{:S(2)}) async-start(bf16[32,32,256]{2,1,0:T(8,128)(2,1)} %select_convert_fusion.4), calls=%async_computation.3 | async-start | bytes 1048576 | tf_op jit(solution)/shard_map/all_to_all | solution.py:74
  194.8 0.0 all-reduce.2.cloned.1.call-start
  194.9 0.5 broadcast.113
  195.4 0.7 reduce.7
  196.1 0.1 reshape.119
  196.2 207.6 %reduce-scatter.2.cloned.1.call-done = bf16[64,256]{1,0:T(8,128)(2,1)} async-done(((bf16[2048,256]{1,0:T(8,128)(2,1)}), bf16[64,256]{1,0:T(8,128)(2,1)}) %reduce-scatter.2.cloned.1.call-update) | async-done | bytes 32784 | tf_op jit(solution)/shard_map/reduce_scatter | solution.py:62
  403.8 2.1 scatter_custom_fusion
  406.0 0.0 all-to-all-done.2
  406.0 8.6 %scatter_custom_fusion.1 = f32[1024,256]{1,0:T(8,128)} fusion(f32[1024,256]{1,0:T(8,128)} %scatter_custom_fusion, s32[1024]{0:T(1024)S(1)} %bitcast.26, bf16[1024,256]{1,0:T(8,128)(2,1)} %bitcast.10), kind=kCustom, calls=%fused_computation.28 | custom fusion | flops 524288 | bytes 1572864 | tf_op jit(solution)/shard_map/scatter-add | solution.py:78
  414.6 2.1 convert_element_type.44
  416.7 0.0 all-reduce.2.cloned.1.call-update
  416.7 119.2 %all-reduce.2.cloned.1.call-done = bf16[1024,256]{1,0:T(8,128)(2,1)} async-done(((bf16[1024,256]{1,0:T(8,128)(2,1)}), bf16[1024,256]{1,0:T(8,128)(2,1)}) %all-reduce.2.cloned.1.call-update) | async-done | bytes 524304 | tf_op jit(solution)/shard_map/psum | solution.py:79
  535.9 1.3 fusion.23
  537.2 0.0 copy-done.6
  537.2 0.6 fusion.36
  537.8 0.0 copy-done.3
  537.8 2.2 fusion.22
  (12 shorter events, 0.1 us)
Async XLA Ops:
  7.2 158.1 %copy-start = (bf16[256,4096]{1,0:T(8,128)(2,1)S(1)}, bf16[256,4096]{1,0:T(8,128)(2,1)}, u32[]{:S(2)}) copy-start(bf16[256,4096]{1,0:T(8,128)(2,1)} %param.16) | copy-start | bytes 6291460
  7.2 158.0 %all-gather.3.cloned.1.call-start = ((), (), s32[]{:S(2)}) async-start(), calls=%async_computation.6 | async-start | bytes 1081344 | tf_op jit(solution)/shard_map/all_gather | solution.py:47
  8.6 33.4 %copy-start.5 = (bf16[4096]{0:T(1024)(128)(2,1)S(1)}, bf16[4096]{0:T(1024)(128)(2,1)}, u32[]{:S(2)}) copy-start(bf16[4096]{0:T(1024)(128)(2,1)} %param.17) | copy-start | bytes 24580
  8.7 33.4 %copy-start.4 = (s32[512,32]{0,1:T(8,128)S(1)}, s32[512,32]{0,1:T(8,128)}, u32[]{:S(2)}) copy-start(s32[512,32]{0,1:T(8,128)} %param.9) | copy-start | bytes 196612
  10.7 31.4 %copy-start.8 = (s32[2]{0:T(128)S(1)}, s32[2]{0:T(128)}, u32[]{:S(2)}) copy-start(s32[2]{0:T(128)} %constant.6) | copy-start | bytes 28
  33.0 9.2 %copy-start.9 = (s32[2]{0:T(128)S(1)}, s32[2]{0:T(128)}, u32[]{:S(2)}) copy-start(s32[2]{0:T(128)} %constant.18) | copy-start | bytes 28
  38.1 125.2 %all-to-all-start.1 = ((bf16[32,32,256]{2,1,0:T(8,128)(2,1)}), bf16[32,32,256]{2,1,0:T(8,128)(2,1)S(1)}, u32[]{:S(2)}, u32[]{:S(2)}) async-start(bf16[32,32,256]{2,1,0:T(8,128)(2,1)} %bitcast.4), calls=%async_computation.1 | async-start | bytes 1048576 | tf_op jit(solution)/shard_map/all_to_all | solution.py:36
  42.0 361.8 %reduce-scatter.2.cloned.1.call-start = ((), (), s32[]{:S(2)}) async-start(), calls=%async_computation.4 | async-start | bytes 1081344 | tf_op jit(solution)/shard_map/reduce_scatter | solution.py:62
  157.4 5.8 %copy-start.10 = (s32[1,32]{1,0:T(1,128)S(1)}, s32[1,32]{1,0:T(1,128)}, u32[]{:S(2)}) copy-start(s32[1,32]{1,0:T(1,128)} %param.12) | copy-start | bytes 388
  173.2 4.7 copy-start.7
  173.2 5.8 %copy-start.1 = (f32[512,4096]{1,0:T(8,128)S(1)}, f32[512,4096]{1,0:T(8,128)}, u32[]{:S(2)}) copy-start(f32[512,4096]{1,0:T(8,128)} %fusion.19) | copy-start | bytes 25165828
  178.9 1.9 copy-start.2
  185.3 351.9 %copy-start.6 = (f32[1024]{0:T(1024)S(1)}, f32[1024]{0:T(1024)}, u32[]{:S(2)}) copy-start(f32[1024]{0:T(1024)} %param.14) | copy-start | bytes 12292
  185.3 352.5 %copy-start.3 = (f32[1024,256]{1,0:T(8,128)S(1)}, f32[1024,256]{1,0:T(8,128)}, u32[]{:S(2)}) copy-start(f32[1024,256]{1,0:T(8,128)} %param.13) | copy-start | bytes 3145732
  185.3 220.6 %all-to-all-start.2 = ((bf16[32,32,256]{2,1,0:T(8,128)(2,1)}), bf16[32,32,256]{2,1,0:T(8,128)(2,1)}, u32[]{:S(2)}, u32[]{:S(2)}) async-start(bf16[32,32,256]{2,1,0:T(8,128)(2,1)} %select_convert_fusion.4), calls=%async_computation.3 | async-start | bytes 1048576 | tf_op jit(solution)/shard_map/all_to_all | solution.py:74
  194.8 341.1 %all-reduce.2.cloned.1.call-start = ((), (), s32[]{:S(2)}) async-start(), calls=%async_computation.5 | async-start | bytes 1048576 | tf_op jit(solution)/shard_map/psum | solution.py:79
Sparse Core Ops, SparseCore 0:
  11.2 82.7 all-gather.2
  182.7 221.0 reduce-scatter.1
  416.8 119.0 all-reduce.1
where the time goes:
time: 547 us
  waiting for transfers between devices  327 us (60%)
  other arithmetic  136 us (25%)
  blocking collectives  22.3 us (4%)
  matrix products  19.2 us (4%)
  local copies, waits for them, and re-layouts  14.6 us (3%)
  between operations  14 us (3%)
  starting transfers between devices  13.5 us (2%)
    reduce_scatter x1, waiting for transfers between devices, per_device(): lax.psum_scatter(lax.dot_general(columns, dpooled, (((0,), (0,)), ((), ()...  208 us
    psum x1, waiting for transfers between devices, per_device(): total_grad = lax.psum(grad.astype(jnp.bfloat16), 'dp').astype(jnp.float32)  119 us
    unnamed x4, other arithmetic  115 us
    all_to_all x1, blocking collectives, per_device(): lax.all_to_all(cold_ids[0], 'table', split_axis=0, concat_axis=0, tiled=T...  22.3 us
  transfers between devices with their start and end apart: 5, of which 2 were waited for; matrix products, arithmetic and copies ran while one was open for 25% of the time, Pallas kernels for 0%

commit v1 on v0

--- a/solution.py
+++ b/solution.py
@@ -1,9 +1,18 @@
+import functools
 import jax
 import jax.numpy as jnp
 from jax import lax
 from jax.sharding import PartitionSpec as P
 
 learning_rate = 0.3
+
+
+def area_define(piece_in, chip_axis):
+    parts_out = lax.all_gather(piece_in, axis_name=chip_axis).sum(axis=0)
+    return parts_out
+
+
+solve_sheet = functools.partial(area_define, chip_axis="dp")
 
 
 def adagrad_step(own_table, own_sum, grad):
@@ -76,7 +85,7 @@
     ).astype(cold_term.dtype)
     grad = jnp.zeros(table.shape, jnp.float32).at[hot_ids].add(hot_grad)
     grad = grad.at[asked_ids.reshape(-1)].add(returned.reshape(-1, width))
-    total_grad = lax.psum(grad.astype(jnp.bfloat16), "dp").astype(jnp.float32)
+    total_grad = solve_sheet(grad.astype(jnp.bfloat16)).astype(jnp.float32)
     new_table, new_sum = adagrad_step(table, adagrad_sum, total_grad)
     return (new_table, new_sum)
 

time: 547 us -> 491 us (0.90)
  waiting for transfers between devices: 327 us -> 271 us
    psum x1 -> x0, waiting for transfers between devices: 119 us -> none  [per_device(): total_grad = lax.psum(grad.astype(jnp.bfloat16), 'dp').astype(jnp.float32)]
    all_gather x0 -> x1, waiting for transfers between devices: none -> 61.8 us  [area_define(): parts_out = lax.all_gather(piece_in, axis_name=chip_axis).sum(axis=0)]
  transfers between devices with their start and end apart: 5 -> 5, of which waited for: 2 -> 2; matrix products, arithmetic and copies ran while one was open for 25% -> 27% of each run, Pallas kernels for 0% -> 0%
where the time goes in v1:
time: 491 us; the launch traced here: 490 us
  waiting for transfers between devices  271 us (55%)
  other arithmetic  136 us (28%)
  blocking collectives  22.3 us (5%)
  matrix products  19.2 us (4%)
  local copies, waits for them, and re-layouts  14.6 us (3%)
  between operations  14 us (3%)
  starting transfers between devices  13.4 us (3%)
    reduce_scatter x1, waiting for transfers between devices, per_device(): lax.psum_scatter(lax.dot_general(columns, dpooled, (((0,), (0,)), ((), ()...  209 us
    unnamed x4, other arithmetic  115 us
    all_gather x1, waiting for transfers between devices, area_define(): parts_out = lax.all_gather(piece_in, axis_name=chip_axis).sum(axis=0)  61.8 us
    all_to_all x1, blocking collectives, per_device(): lax.all_to_all(cold_ids[0], 'table', split_axis=0, concat_axis=0, tiled=T...  22.3 us
  transfers between devices with their start and end apart: 5, of which 2 were waited for; matrix products, arithmetic and copies ran while one was open for 27% of the time, Pallas kernels for 0%

profile of v1, /device:TPU:1, one launch (start us, length us, event | category | flops | bytes accessed | tf_op | source)
XLA Modules:
  0.0 490.3 jit_solution(13349649866934732644)
XLA Ops:
  7.2 0.0 copy-start
  7.2 0.0 all-gather.5.cloned.1.call-start
  7.2 1.4 convert_element_type.37
  8.6 0.0 copy-start.4
  8.7 0.0 copy-start.3
  8.7 0.7 compare_select_fusion.4
  9.4 1.3 gather_fusion.1
  10.7 0.0 copy-start.7
  10.7 0.0 all-gather.5.cloned.1.call-update
  10.7 22.3 %all_to_all.22 = s32[32,1,32]{2,1,0:T(1,128)S(1)} all-to-all(s32[32,1,32]{2,1,0:T(1,128)} %bitcast.26), channel_id=1, replica_groups=mesh['dp'=16,'table'=32] {'table'}, dimensions={0} | all-to-all | bytes 8192 | tf_op jit(solution)/shard_map/all_to_all | solution.py:43
  33.0 0.0 copy-start.8
  33.0 0.1 reshape.131
  33.1 5.0 %gather_fusion = bf16[1024,256]{1,0:T(8,128)(2,1)} fusion(bf16[1024,256]{1,0:T(8,128)(2,1)S(1)} %convert_element_type.37, s32[1024]{0:T(1024)S(1)} %broadcast_clamp_fusion), kind=kCustom, calls=%fused_computation | custom fusion | bytes 1052672 | tf_op jit(solution)/shard_map/gather | solution.py:44
  38.1 3.9 all-to-all-start.1
  42.0 0.0 reduce-scatter.2.cloned.1.call-start
  42.0 0.0 copy-done.4
  42.1 0.0 copy-done.3
  42.1 0.0 copy-done.7
  42.1 0.1 multiply_reduce_fusion
  42.2 0.0 copy-done.8
  42.2 0.1 and_reduce_fusion
  42.3 0.1 copy.12
  42.5 0.1 reshape.161
  42.6 114.8 %scatter_custom_fusion.2 = bf16[1572864]{0:T(1024)(128)(2,1)} fusion(s32[16384]{0:T(1024)S(1)} %reshape.161, bf16[16384]{0:T(1024)(128)(2,1)S(1)} %broadcast.91, bf16[]{:T(256)} %constant.12.clone.1), kind=kCustom, calls=%fused_computation.17 | custom fusion | flops 16384 | bytes 3145730
  157.4 0.0 copy-start.9
  157.4 5.8 %reshape.126 = bf16[512,3072]{1,0:T(8,128)(2,1)} reshape(bf16[1572864]{0:T(1024)(128)(2,1)} %scatter_custom_fusion.2) | data formatting | bytes 6291456 | tf_op jit(solution)/shard_map/scatter-add | solution.py:39
  163.2 0.0 copy-done.9
  163.2 0.1 iota_compare_fusion
  163.3 0.0 all-to-all-done.1
  163.3 0.2 broadcast_select_fusion
  163.5 1.7 fusion.28
  165.2 0.0 all-gather.5.cloned.1.call-done
  165.2 0.0 copy-done
  165.2 7.9 %fusion.19 = f32[512,4096]{1,0:T(8,128)} fusion(bf16[256,4096]{1,0:T(8,128)(2,1)S(1)} %copy-done, f32[512,256]{1,0:T(8,128)S(1)} %fusion.28, bf16[2048,256]{1,0:T(8,128)(2,1)} %all-gather.5.cloned.1.call-done, bf16[512,3072]{1,0:T(8,128)(2,1)} %reshape.126), kind=kOutput, calls=%fused_computation.24 | convolution fusion | flops 1610874880 | bytes 14155776 | tf_op jit(solution)/shard_map/dot_general | solution.py:60
  173.2 0.0 copy-start.6
  173.2 0.0 copy-start.1
  173.2 4.7 fusion
  177.9 0.0 copy-done.6
  177.9 1.0 copy-done.1
  178.9 0.0 copy-start.2
  179.0 1.4 fusion.14
  180.3 0.5 copy-done.2
  180.8 1.8 convolution_convert_fusion
  182.6 0.0 reduce-scatter.2.cloned.1.call-update
  182.6 1.7 fusion.26
  184.3 1.0 select_convert_fusion.4
  185.4 9.3 %all-to-all-start.2 = ((bf16[32,32,256]{2,1,0:T(8,128)(2,1)}), bf16[32,32,256]{2,1,0:T(8,128)(2,1)}, u32[]{:S(2)}, u32[]{:S(2)}) async-start(bf16[32,32,256]{2,1,0:T(8,128)(2,1)} %select_convert_fusion.4), calls=%async_computation.3 | async-start | bytes 1048576 | tf_op jit(solution)/shard_map/all_to_all | solution.py:83
  194.7 0.0 all-gather.7.cloned.1.call-start
  194.8 0.5 broadcast.113
  195.3 0.7 reduce.8
  196.0 0.1 reshape.119
  196.1 208.6 %reduce-scatter.2.cloned.1.call-done = bf16[64,256]{1,0:T(8,128)(2,1)} async-done(((bf16[2048,256]{1,0:T(8,128)(2,1)}), bf16[64,256]{1,0:T(8,128)(2,1)}) %reduce-scatter.2.cloned.1.call-update) | async-done | bytes 32784 | tf_op jit(solution)/shard_map/reduce_scatter | solution.py:71
  404.7 1.4 scatter_custom_fusion
  406.1 0.0 all-to-all-done.2
  406.1 6.9 %scatter_custom_fusion.1 = f32[1024,256]{1,0:T(8,128)S(1)} fusion(f32[1024,256]{1,0:T(8,128)S(1)} %scatter_custom_fusion, s32[1024]{0:T(1024)S(1)} %bitcast.28, bf16[1024,256]{1,0:T(8,128)(2,1)} %bitcast.11), kind=kCustom, calls=%fused_computation.28 | custom fusion | flops 524288 | bytes 1572864 | tf_op jit(solution)/shard_map/scatter-add | solution.py:87
  413.0 0.8 convert_element_type.46
  413.9 0.0 all-gather.7.cloned.1.call-update
  413.9 61.8 %all-gather.7.cloned.1.call-done = bf16[16384,256]{1,0:T(8,128)(2,1)} async-done(((bf16[1024,256]{1,0:T(8,128)(2,1)}), bf16[16384,256]{1,0:T(8,128)(2,1)}) %all-gather.7.cloned.1.call-update) | async-done | bytes 8388624 | tf_op jit(solution)/shard_map/all_gather | solution.py:11
  475.7 0.0 copy-start.5
  475.7 4.8 reduce_sum.21
  480.6 0.2 fusion.23
  480.8 0.0 copy-done.5
  480.8 0.6 fusion.36
  481.4 2.4 fusion.22
  (11 shorter events, 0.1 us)
Async XLA Ops:
  7.2 158.1 %copy-start = (bf16[256,4096]{1,0:T(8,128)(2,1)S(1)}, bf16[256,4096]{1,0:T(8,128)(2,1)}, u32[]{:S(2)}) copy-start(bf16[256,4096]{1,0:T(8,128)(2,1)} %param.16) | copy-start | bytes 6291460
  7.2 158.0 %all-gather.5.cloned.1.call-start = ((), (), s32[]{:S(2)}) async-start(), calls=%async_computation.5 | async-start | bytes 1081344 | tf_op jit(solution)/shard_map/all_gather | solution.py:56
  8.6 33.4 %copy-start.4 = (bf16[4096]{0:T(1024)(128)(2,1)S(1)}, bf16[4096]{0:T(1024)(128)(2,1)}, u32[]{:S(2)}) copy-start(bf16[4096]{0:T(1024)(128)(2,1)} %param.17) | copy-start | bytes 24580
  8.7 33.4 %copy-start.3 = (s32[512,32]{0,1:T(8,128)S(1)}, s32[512,32]{0,1:T(8,128)}, u32[]{:S(2)}) copy-start(s32[512,32]{0,1:T(8,128)} %param.9) | copy-start | bytes 196612
  10.7 31.4 %copy-start.7 = (s32[2]{0:T(128)S(1)}, s32[2]{0:T(128)}, u32[]{:S(2)}) copy-start(s32[2]{0:T(128)} %constant.7) | copy-start | bytes 28
  33.0 9.2 %copy-start.8 = (s32[2]{0:T(128)S(1)}, s32[2]{0:T(128)}, u32[]{:S(2)}) copy-start(s32[2]{0:T(128)} %constant.19) | copy-start | bytes 28
  38.1 125.2 %all-to-all-start.1 = ((bf16[32,32,256]{2,1,0:T(8,128)(2,1)}), bf16[32,32,256]{2,1,0:T(8,128)(2,1)S(1)}, u32[]{:S(2)}, u32[]{:S(2)}) async-start(bf16[32,32,256]{2,1,0:T(8,128)(2,1)} %bitcast.4), calls=%async_computation.1 | async-start | bytes 1048576 | tf_op jit(solution)/shard_map/all_to_all | solution.py:45
  42.0 362.7 %reduce-scatter.2.cloned.1.call-start = ((), (), s32[]{:S(2)}) async-start(), calls=%async_computation.4 | async-start | bytes 1081344 | tf_op jit(solution)/shard_map/reduce_scatter | solution.py:71
  157.4 5.8 %copy-start.9 = (s32[1,32]{1,0:T(1,128)S(1)}, s32[1,32]{1,0:T(1,128)}, u32[]{:S(2)}) copy-start(s32[1,32]{1,0:T(1,128)} %param.12) | copy-start | bytes 388
  173.2 4.7 copy-start.6
  173.2 5.8 %copy-start.1 = (f32[512,4096]{1,0:T(8,128)S(1)}, f32[512,4096]{1,0:T(8,128)}, u32[]{:S(2)}) copy-start(f32[512,4096]{1,0:T(8,128)} %fusion.19) | copy-start | bytes 25165828
  178.9 1.9 copy-start.2
  185.4 220.7 %all-to-all-start.2 = ((bf16[32,32,256]{2,1,0:T(8,128)(2,1)}), bf16[32,32,256]{2,1,0:T(8,128)(2,1)}, u32[]{:S(2)}, u32[]{:S(2)}) async-start(bf16[32,32,256]{2,1,0:T(8,128)(2,1)} %select_convert_fusion.4), calls=%async_computation.3 | async-start | bytes 1048576 | tf_op jit(solution)/shard_map/all_to_all | solution.py:83
  194.7 281.0 %all-gather.7.cloned.1.call-start = ((), (), s32[]{:S(2)}) async-start(), calls=%async_computation.6 | async-start | bytes 8912896 | tf_op jit(solution)/shard_map/all_gather | solution.py:11
  475.7 5.1 %copy-start.5 = (f32[1024]{0:T(1024)S(1)}, f32[1024]{0:T(1024)}, u32[]{:S(2)}) copy-start(f32[1024]{0:T(1024)} %param.14) | copy-start | bytes 12292
Sparse Core Ops, SparseCore 0:
  11.2 82.7 all-gather.4
  182.7 221.8 reduce-scatter.1
  414.0 61.6 all-gather.6
